TPU v7x, 256 devices: a whole 4x4x8 slice. The times are simulated.
256 devices in a mesh: grp: 8 (over z_hi, y), row: 32 (over z_lo, x, core).
Axes of the slice: x: 4, y: 4, z: 8 (z_hi: 2, z_lo: 4; z = z_hi * 4 + z_lo), core: 2. Of those that a mesh axis runs over, the one named last changes fastest.
Arguments:
- points: bfloat16 [524288, 128], P(('grp', 'row')), as said below
- centers: bfloat16 [8192, 128], replicated, as said below
- inner_factor: bfloat16 [8192, 8192], P('row'), as said below
- outer_factor: bfloat16 [8192, 8192], P('row'), as said below
- iterate: float32 [64, 8192], P(None, 'row'), may hold values from -6 to 6
- residual: float32 [64, 8192], P(None, 'row'), as said below
- direction: float32 [64, 8192], P(None, 'row'), as said below
Outputs:
- next_iterate: float32 [64, 8192], P(None, 'row')
- next_residual: float32 [64, 8192], P(None, 'row')
- next_direction: float32 [64, 8192], P(None, 'row')
Inputs may be any that keep to these rules, and one draw needn't show every extreme that they name: `inner_factor`: upper triangular: zero below the diagonal, positive on it. `outer_factor`: upper triangular: zero below the diagonal, positive on it. `residual`: finite real values. `direction`: finite real values. `points`: finite real values. `centers`: finite real values.
All inputs are finite; a program needn't handle non-finite values.
Results may differ from a plain program's by a relative error of at most 0.0056.
Values may be sent and summed in bfloat16 or wider, within the bound.
No kernel may reach another device: no remote copies, remote signals or barrier semaphores. Data moves between devices by JAX's collectives and lax.ppermute only.
A program may use at most 64 MiB of HBM per device.

v0:
```python
import jax
import jax.numpy as jnp
from jax import lax
from jax.sharding import PartitionSpec as P

ridge_weight = 0.5


def kernel_rows(block_points, centers, center_norms):
    point_wide = block_points.astype(jnp.float32)
    point_norms = jnp.sum(point_wide * point_wide, axis=1)
    cross_term = lax.dot_general(
        block_points, centers, (((1,), (1,)), ((), ())), preferred_element_type=jnp.float32
    )
    distance = point_norms[:, None] + center_norms[None, :] - 2.0 * cross_term
    return jnp.exp(distance * (-4.0 / block_points.shape[1])).astype(jnp.bfloat16)


def local(points, centers, inner_factor, outer_factor, iterate, residual, direction):
    contract_last = (((1,), (1,)), ((), ()))
    own_rows = inner_factor.shape[0]
    targets = direction.shape[0]
    direction_half = direction.astype(jnp.bfloat16)
    columns = inner_factor
    inner_term = lax.dot_general(
        lax.all_gather(direction_half, "row", axis=1, tiled=True),
        columns,
        contract_last,
        preferred_element_type=jnp.float32,
    )
    inner_half = inner_term.astype(jnp.bfloat16)
    columns = outer_factor
    outer_rows = lax.dot_general(
        lax.all_gather(inner_half, "row", axis=1, tiled=True),
        columns,
        contract_last,
        preferred_element_type=jnp.float32,
    )
    outer_half = lax.all_gather(outer_rows.astype(jnp.bfloat16), "row", axis=1, tiled=True)
    center_wide = centers.astype(jnp.float32)
    center_norms = jnp.sum(center_wide * center_wide, axis=1)
    local_points = points.shape[0]
    block_rows = min(512, local_points)
    point_blocks = points.reshape(local_points // block_rows, block_rows, points.shape[1])

    def one_block(carried, block_points):
        kernel_block = kernel_rows(block_points, centers, center_norms)
        fitted = lax.dot_general(
            outer_half, kernel_block, contract_last, preferred_element_type=jnp.float32
        ).astype(jnp.bfloat16)
        return (carried + jnp.dot(fitted, kernel_block, preferred_element_type=jnp.float32), None)

    partial_sums, _ = lax.scan(
        one_block, jnp.zeros((targets, centers.shape[0]), jnp.float32), point_blocks
    )
    summed_all = lax.psum(partial_sums, ("grp", "row"))
    own_normal = lax.dynamic_slice_in_dim(summed_all, lax.axis_index("row") * own_rows, own_rows, 1)
    normal_half = own_normal.astype(jnp.bfloat16)
    point_count = local_points * lax.axis_size("grp") * lax.axis_size("row")
    outer_terms = jnp.dot(normal_half, outer_factor, preferred_element_type=jnp.float32)
    shaped = (
        lax.psum_scatter(outer_terms, "row", scatter_dimension=1, tiled=True) / point_count
        + ridge_weight * inner_term
    )
    shaped_half = shaped.astype(jnp.bfloat16)
    inner_terms = jnp.dot(shaped_half, inner_factor, preferred_element_type=jnp.float32)
    operator_image = lax.psum_scatter(inner_terms, "row", scatter_dimension=1, tiled=True)
    old_norm = lax.psum(jnp.sum(residual * residual, axis=1), "row")
    curvature = lax.psum(jnp.sum(direction * operator_image, axis=1), "row")
    step_size = old_norm / curvature
    next_residual = residual - step_size[:, None] * operator_image
    new_norm = lax.psum(jnp.sum(next_residual * next_residual, axis=1), "row")
    next_iterate = iterate + step_size[:, None] * direction
    next_direction = next_residual + (new_norm / old_norm)[:, None] * direction
    return (next_iterate, next_residual, next_direction)


def solution(mesh):
    placed = (
        P(("grp", "row"), None),
        P(),
        P("row", None),
        P("row", None),
        P(None, "row"),
        P(None, "row"),
        P(None, "row"),
    )
    return jax.shard_map(
        local,
        mesh=mesh,
        in_specs=placed,
        out_specs=(P(None, "row"), P(None, "row"), P(None, "row")),
        check_vma=False,
    )
```

profile of v0, /device:TPU:1, one launch (start us, length us, event | category | flops | bytes accessed | tf_op | source)
XLA Modules:
  0.0 819.4 jit_solution(775019206389307324)
XLA Ops:
  7.2 1.5 convert_element_type.29
  8.7 66.0 %all-gather.4.cloned.1.call-done = bf16[64,8192]{1,0:T(8,128)(2,1)} async-done(((bf16[64,256]{1,0:T(8,128)(2,1)}), bf16[64,8192]{1,0:T(8,128)(2,1)}) %all-gather.4.cloned.1.call-update) | async-done | bytes 1048592 | tf_op jit(solution)/shard_map/all_gather | solution.py:26
  74.8 4.5 fusion.10
  79.4 59.4 %all-gather.6.cloned.1.call-done = bf16[64,8192]{1,0:T(8,128)(2,1)} async-done(((bf16[64,256]{1,0:T(8,128)(2,1)}), bf16[64,8192]{1,0:T(8,128)(2,1)}) %all-gather.6.cloned.1.call-update) | async-done | bytes 1048592 | tf_op jit(solution)/shard_map/all_gather | solution.py:34
  138.7 4.5 convolution_convert_fusion.1
  143.5 2.7 multiply_reduce_fusion.1
  146.3 56.4 %all-gather.8.cloned.1.call-done = bf16[64,8192]{1,0:T(8,128)(2,1)} async-done(((bf16[64,256]{1,0:T(8,128)(2,1)}), bf16[64,8192]{1,0:T(8,128)(2,1)}) %all-gather.8.cloned.1.call-update) | async-done | bytes 1048592 | tf_op jit(solution)/shard_map/all_gather | solution.py:39
  202.7 87.9 %while.11 = (s32[]{:T(128)}, f32[64,8192]{1,0:T(8,128)S(1)}, bf16[4,512,128]{2,1,0:T(8,128)(2,1)}, f32[8192]{0:T(1024)S(1)}, bf16[8192,128]{1,0:T(8,128)(2,1)}, ...) while((s32[]{:T(128)}, f32[64,8192]{1,0:T(8,128)S(1)}, bf16[4,512,128]{2,1,0:T(8,128)(2,1)}, ...), condition=%wide.region_5.6_spmd.clone, body=%wide.region_3.0_spmd.clone.sunk | while | flops 2169732608 | bytes 28610700 | solution.py:53
  203.7 9.0 %exponential_convert_fusion.2 = bf16[512,8192]{1,0:T(8,128)(2,1)} fusion(bf16[8192,128]{1,0:T(8,128)(2,1)} %get-tuple-element.134, f32[8192]{0:T(1024)S(1)} %get-tuple-element.133, f32[512]{0:T(512)S(1)} %multiply_reduce_fusion.6, bf16[4,512,128]{2,1,0:T(8,128)(2,1)} %get-tuple-element.132, s32[]{:T(128)S(6)} %copy.12), kind=kOutput, calls=%fused_computation.clone.1 | convolution fusion | flops 1094713344 | bytes 10651652 | tf_op jit(solution)/shard_map/while/body/eval_jaxpr/dot_general | solution.py:12
  212.8 11.9 %convolution_add_fusion.2 = f32[64,8192]{1,0:T(8,128)S(1)} fusion(bf16[512,8192]{1,0:T(8,128)(2,1)} %exponential_convert_fusion.2, f32[64,8192]{1,0:T(8,128)S(1)} %get-tuple-element.123, pred[]{:T(512)S(6)} %compare.3, bf16[64,8192]{1,0:T(8,128)(2,1)S(1)} %copy-done), kind=kOutput, calls=%fused_computation.1.clone.1 | convolution fusion | flops 1074823168 | bytes 13631489 | tf_op jit(solution)/shard_map/while/body/eval_jaxpr/dot_general | solution.py:51
  224.7 1.1 multiply_reduce_fusion.6
  225.7 9.0 %exponential_convert_fusion.2 = bf16[512,8192]{1,0:T(8,128)(2,1)} fusion(bf16[8192,128]{1,0:T(8,128)(2,1)} %get-tuple-element.134, f32[8192]{0:T(1024)S(1)} %get-tuple-element.133, f32[512]{0:T(512)S(1)} %multiply_reduce_fusion.6, bf16[4,512,128]{2,1,0:T(8,128)(2,1)} %get-tuple-element.132, s32[]{:T(128)S(6)} %copy.12), kind=kOutput, calls=%fused_computation.clone.1 | convolution fusion | flops 1094713344 | bytes 10651652 | tf_op jit(solution)/shard_map/while/body/eval_jaxpr/dot_general | solution.py:12
  234.8 11.9 %convolution_add_fusion.2 = f32[64,8192]{1,0:T(8,128)S(1)} fusion(bf16[512,8192]{1,0:T(8,128)(2,1)} %exponential_convert_fusion.2, f32[64,8192]{1,0:T(8,128)S(1)} %get-tuple-element.123, pred[]{:T(512)S(6)} %compare.3, bf16[64,8192]{1,0:T(8,128)(2,1)S(1)} %copy-done), kind=kOutput, calls=%fused_computation.1.clone.1 | convolution fusion | flops 1074823168 | bytes 13631489 | tf_op jit(solution)/shard_map/while/body/eval_jaxpr/dot_general | solution.py:51
  247.7 9.0 %exponential_convert_fusion.2 = bf16[512,8192]{1,0:T(8,128)(2,1)} fusion(bf16[8192,128]{1,0:T(8,128)(2,1)} %get-tuple-element.134, f32[8192]{0:T(1024)S(1)} %get-tuple-element.133, f32[512]{0:T(512)S(1)} %multiply_reduce_fusion.6, bf16[4,512,128]{2,1,0:T(8,128)(2,1)} %get-tuple-element.132, s32[]{:T(128)S(6)} %copy.12), kind=kOutput, calls=%fused_computation.clone.1 | convolution fusion | flops 1094713344 | bytes 10651652 | tf_op jit(solution)/shard_map/while/body/eval_jaxpr/dot_general | solution.py:12
  256.7 11.9 %convolution_add_fusion.2 = f32[64,8192]{1,0:T(8,128)S(1)} fusion(bf16[512,8192]{1,0:T(8,128)(2,1)} %exponential_convert_fusion.2, f32[64,8192]{1,0:T(8,128)S(1)} %get-tuple-element.123, pred[]{:T(512)S(6)} %compare.3, bf16[64,8192]{1,0:T(8,128)(2,1)S(1)} %copy-done), kind=kOutput, calls=%fused_computation.1.clone.1 | convolution fusion | flops 1074823168 | bytes 13631489 | tf_op jit(solution)/shard_map/while/body/eval_jaxpr/dot_general | solution.py:51
  269.7 9.0 %exponential_convert_fusion.2 = bf16[512,8192]{1,0:T(8,128)(2,1)} fusion(bf16[8192,128]{1,0:T(8,128)(2,1)} %get-tuple-element.134, f32[8192]{0:T(1024)S(1)} %get-tuple-element.133, f32[512]{0:T(512)S(1)} %multiply_reduce_fusion.6, bf16[4,512,128]{2,1,0:T(8,128)(2,1)} %get-tuple-element.132, s32[]{:T(128)S(6)} %copy.12), kind=kOutput, calls=%fused_computation.clone.1 | convolution fusion | flops 1094713344 | bytes 10651652 | tf_op jit(solution)/shard_map/while/body/eval_jaxpr/dot_general | solution.py:12
  278.7 11.9 %convolution_add_fusion.2 = f32[64,8192]{1,0:T(8,128)S(1)} fusion(bf16[512,8192]{1,0:T(8,128)(2,1)} %exponential_convert_fusion.2, f32[64,8192]{1,0:T(8,128)S(1)} %get-tuple-element.123, pred[]{:T(512)S(6)} %compare.3, bf16[64,8192]{1,0:T(8,128)(2,1)S(1)} %copy-done), kind=kOutput, calls=%fused_computation.1.clone.1 | convolution fusion | flops 1074823168 | bytes 13631489 | tf_op jit(solution)/shard_map/while/body/eval_jaxpr/dot_general | solution.py:51
  290.6 85.9 %all-reduce.2 = bf16[64,8192]{1,0:T(8,128)(2,1)S(1)} all-reduce(f32[64,8192]{1,0:T(8,128)S(1)} %get-tuple-element.35), channel_id=1, replica_groups=mesh['grp'=8,'row'=32] {'grp','row'}, use_global_device_ids=true, to_apply=%region_6.7 | all-reduce | flops 524288 | bytes 3145728 | tf_op jit(solution)/shard_map/psum | solution.py:56
  376.5 4.4 fusion.3
  380.9 139.3 %reduce-scatter.3.cloned.1.call-done = f32[64,256]{1,0:T(8,128)} async-done(((f32[64,8192]{1,0:T(8,128)}), f32[64,256]{1,0:T(8,128)}) %reduce-scatter.3.cloned.1.call-update) | async-done | bytes 65552 | tf_op jit(solution)/shard_map/reduce_scatter | solution.py:62
  520.3 4.5 fusion.4
  524.9 144.8 %reduce-scatter.5.cloned.1.call-done = f32[64,256]{1,0:T(8,128)} async-done(((f32[64,8192]{1,0:T(8,128)}), f32[64,256]{1,0:T(8,128)}) %reduce-scatter.5.cloned.1.call-update) | async-done | bytes 65552 | tf_op jit(solution)/shard_map/reduce_scatter | solution.py:67
  670.7 72.6 %all-reduce = (f32[64]{0:T(128)S(1)}, f32[64]{0:T(128)S(1)}) all-reduce(f32[64]{0:T(128)S(1)} %multiply_reduce_fusion.4, f32[64]{0:T(128)S(1)} %multiply_reduce_fusion.3), channel_id=1, replica_groups=mesh['grp'=8,'row'=32] {'row'}, use_global_device_ids=true, to_apply=%region_1.2 | all-reduce | flops 128 | bytes 1024 | tf_op jit(solution)/shard_map/psum | solution.py:68
  744.3 67.9 %psum.31 = f32[64]{0:T(128)S(1)} all-reduce(f32[64]{0:T(128)S(1)} %get-tuple-element.71), channel_id=1, replica_groups=mesh['grp'=8,'row'=32] {'row'}, use_global_device_ids=true, to_apply=%region_12.13 | all-reduce | flops 64 | bytes 512 | tf_op jit(solution)/shard_map/psum | solution.py:72
  (36 shorter events, 6.5 us)
Async XLA Ops:
  7.2 67.6 %all-gather.4.cloned.1.call-start = ((), (), s32[]{:S(2)}) async-start(), calls=%async_computation.2 | async-start | bytes 1081344 | tf_op jit(solution)/shard_map/all_gather | solution.py:26
  8.7 130.0 %all-gather.6.cloned.1.call-start = ((), (), s32[]{:S(2)}) async-start(), calls=%async_computation.3 | async-start | bytes 1081344 | tf_op jit(solution)/shard_map/all_gather | solution.py:34
  79.3 123.4 %all-gather.8.cloned.1.call-start = ((), (), s32[]{:S(2)}) async-start(), calls=%async_computation.4 | async-start | bytes 1081344 | tf_op jit(solution)/shard_map/all_gather | solution.py:39
  143.3 377.0 %reduce-scatter.3.cloned.1.call-start = ((), (), s32[]{:S(2)}) async-start(), calls=%async_computation.5 | async-start | bytes 2162688 | tf_op jit(solution)/shard_map/reduce_scatter | solution.py:62
  203.7 9.1 %copy-start = (bf16[64,8192]{1,0:T(8,128)(2,1)S(1)}, bf16[64,8192]{1,0:T(8,128)(2,1)}, u32[]{:S(2)}) copy-start(bf16[64,8192]{1,0:T(8,128)(2,1)} %get-tuple-element.135) | copy-start | bytes 3145732 | tf_op jit(solution)/shard_map/while
  225.7 9.1 %copy-start = (bf16[64,8192]{1,0:T(8,128)(2,1)S(1)}, bf16[64,8192]{1,0:T(8,128)(2,1)}, u32[]{:S(2)}) copy-start(bf16[64,8192]{1,0:T(8,128)(2,1)} %get-tuple-element.135) | copy-start | bytes 3145732 | tf_op jit(solution)/shard_map/while
  247.7 9.1 %copy-start = (bf16[64,8192]{1,0:T(8,128)(2,1)S(1)}, bf16[64,8192]{1,0:T(8,128)(2,1)}, u32[]{:S(2)}) copy-start(bf16[64,8192]{1,0:T(8,128)(2,1)} %get-tuple-element.135) | copy-start | bytes 3145732 | tf_op jit(solution)/shard_map/while
  269.7 9.1 %copy-start = (bf16[64,8192]{1,0:T(8,128)(2,1)S(1)}, bf16[64,8192]{1,0:T(8,128)(2,1)}, u32[]{:S(2)}) copy-start(bf16[64,8192]{1,0:T(8,128)(2,1)} %get-tuple-element.135) | copy-start | bytes 3145732 | tf_op jit(solution)/shard_map/while
  380.9 288.8 %reduce-scatter.5.cloned.1.call-start = ((), (), s32[]{:S(2)}) async-start(), calls=%async_computation.6 | async-start | bytes 2162688 | tf_op jit(solution)/shard_map/reduce_scatter | solution.py:67
  520.3 4.5 copy-start.3
  520.3 149.4 %copy-start.1 = (f32[64,256]{1,0:T(8,128)S(1)}, f32[64,256]{1,0:T(8,128)}, u32[]{:S(2)}) copy-start(f32[64,256]{1,0:T(8,128)} %param.15) | copy-start | bytes 196612
  520.3 291.8 %copy-start.4 = (f32[64,256]{1,0:T(8,128)S(1)}, f32[64,256]{1,0:T(8,128)}, u32[]{:S(2)}) copy-start(f32[64,256]{1,0:T(8,128)} %param.13) | copy-start | bytes 196612
  744.3 68.6 %copy-start.2 = (f32[64,256]{1,0:T(8,128)}, f32[64,256]{1,0:T(8,128)S(1)}, u32[]{:S(2)}) copy-start(f32[64,256]{1,0:T(8,128)S(1)} %get-tuple-element.72) | copy-start | bytes 196612
Sparse Core Ops, SparseCore 0:
  10.3 64.4 all-gather.3
  79.4 59.2 all-gather.5
  143.4 59.2 all-gather.7
  381.0 139.2 reduce-scatter.2
  524.9 144.7 reduce-scatter.4
where the time goes:
time: 820 us; the launch traced here: 819 us
  waiting for transfers between devices  466 us (57%)
  blocking collectives  226 us (28%)
  matrix products  101 us (12%)
  between operations  13.8 us (2%)
  other arithmetic  11.2 us (1%)
    reduce_scatter x1, waiting for transfers between devices, local(): lax.psum_scatter(inner_terms, 'row', scatter_dimension=1, tiled=True)  145 us
    reduce_scatter x1, waiting for transfers between devices, local(): lax.psum_scatter(outer_terms, 'row', scatter_dimension=1, tiled=True)  139 us
    psum x1, blocking collectives, local(): summed_all = lax.psum(partial_sums, ('grp', 'row'))  85.9 us
    psum x1, blocking collectives, local(): old_norm = lax.psum(jnp.sum(residual * residual, axis=1), 'row')  72.6 us
    psum x1, blocking collectives, local(): new_norm = lax.psum(jnp.sum(next_residual * next_residual, axis=1), 'row')  67.9 us
    all_gather x1, waiting for transfers between devices, local(): lax.all_gather(direction_half, 'row', axis=1, tiled=True)  66 us
    all_gather x1, waiting for transfers between devices, local(): lax.all_gather(inner_half, 'row', axis=1, tiled=True)  59.4 us
    all_gather x1, waiting for transfers between devices, local(): lax.all_gather(outer_rows.astype(jnp.bfloat16), 'row', axis=1, tiled=True)  56.4 us
  transfers between devices with their start and end apart: 5, of which 5 were waited for; matrix products, arithmetic and copies ran while one was open for 0% of the time, Pallas kernels for 0%

commit v1 on v0

--- a/solution.py
+++ b/solution.py
@@ -53,7 +53,7 @@
     partial_sums, _ = lax.scan(
         one_block, jnp.zeros((targets, centers.shape[0]), jnp.float32), point_blocks
     )
-    summed_all = lax.psum(partial_sums, ("grp", "row"))
+    summed_all = lax.psum(lax.psum(partial_sums, "row"), "grp")
     own_normal = lax.dynamic_slice_in_dim(summed_all, lax.axis_index("row") * own_rows, own_rows, 1)
     normal_half = own_normal.astype(jnp.bfloat16)
     point_count = local_points * lax.axis_size("grp") * lax.axis_size("row")

time: 820 us -> 1130 us (1.38)
  waiting for transfers between devices: 466 us -> 760 us
  blocking collectives: 226 us -> 246 us
    psum x0 -> x1, waiting for transfers between devices: none -> 283 us  [local(): summed_all = lax.psum(lax.psum(partial_sums, 'row'), 'grp')]
    psum x1, blocking collectives: 85.9 us -> 106 us  [local(): summed_all = lax.psum(lax.psum(partial_sums, 'row'), 'grp')]
  transfers between devices with their start and end apart: 5 -> 6, of which waited for: 5 -> 6; matrix products, arithmetic and copies ran while one was open for 0% -> 0% of each run, Pallas kernels for 0% -> 0%
where the time goes in v1:
time: 1130 us
  waiting for transfers between devices  760 us (67%)
  blocking collectives  246 us (22%)
  matrix products  101 us (9%)
  between operations  14.2 us (1%)
    psum x1, waiting for transfers between devices, local(): summed_all = lax.psum(lax.psum(partial_sums, 'row'), 'grp')  283 us
    reduce_scatter x1, waiting for transfers between devices, local(): lax.psum_scatter(outer_terms, 'row', scatter_dimension=1, tiled=True)  150 us
    reduce_scatter x1, waiting for transfers between devices, local(): lax.psum_scatter(inner_terms, 'row', scatter_dimension=1, tiled=True)  145 us
    psum x1, blocking collectives, local(): summed_all = lax.psum(lax.psum(partial_sums, 'row'), 'grp')  106 us
    psum x1, blocking collectives, local(): old_norm = lax.psum(jnp.sum(residual * residual, axis=1), 'row')  72.6 us
    psum x1, blocking collectives, local(): new_norm = lax.psum(jnp.sum(next_residual * next_residual, axis=1), 'row')  67.8 us
    all_gather x1, waiting for transfers between devices, local(): lax.all_gather(direction_half, 'row', axis=1, tiled=True)  66 us
    all_gather x1, waiting for transfers between devices, local(): lax.all_gather(inner_half, 'row', axis=1, tiled=True)  59.4 us
  transfers between devices with their start and end apart: 6, of which 6 were waited for; matrix products, arithmetic and copies ran while one was open for 0% of the time, Pallas kernels for 0%

profile of v1, /device:TPU:1, one launch (start us, length us, event | category | flops | bytes accessed | tf_op | source)
XLA Modules:
  0.0 1134.5 jit_solution(246825405639956224)
XLA Ops:
  7.2 1.5 convert_element_type.29
  8.7 66.0 %all-gather.4.cloned.1.call-done = bf16[64,8192]{1,0:T(8,128)(2,1)} async-done(((bf16[64,256]{1,0:T(8,128)(2,1)}), bf16[64,8192]{1,0:T(8,128)(2,1)}) %all-gather.4.cloned.1.call-update) | async-done | bytes 1048592 | tf_op jit(solution)/shard_map/all_gather | solution.py:26
  74.8 4.5 fusion.10
  79.4 59.4 %all-gather.6.cloned.1.call-done = bf16[64,8192]{1,0:T(8,128)(2,1)} async-done(((bf16[64,256]{1,0:T(8,128)(2,1)}), bf16[64,8192]{1,0:T(8,128)(2,1)}) %all-gather.6.cloned.1.call-update) | async-done | bytes 1048592 | tf_op jit(solution)/shard_map/all_gather | solution.py:34
  138.7 4.5 convolution_convert_fusion.1
  143.3 2.7 multiply_reduce_fusion.1
  146.1 56.6 %all-gather.8.cloned.1.call-done = bf16[64,8192]{1,0:T(8,128)(2,1)} async-done(((bf16[64,256]{1,0:T(8,128)(2,1)}), bf16[64,8192]{1,0:T(8,128)(2,1)}) %all-gather.8.cloned.1.call-update) | async-done | bytes 1048592 | tf_op jit(solution)/shard_map/all_gather | solution.py:39
  202.7 87.9 %while.11 = (s32[]{:T(128)}, f32[64,8192]{1,0:T(8,128)S(1)}, bf16[4,512,128]{2,1,0:T(8,128)(2,1)}, f32[8192]{0:T(1024)S(1)}, bf16[8192,128]{1,0:T(8,128)(2,1)}, ...) while((s32[]{:T(128)}, f32[64,8192]{1,0:T(8,128)S(1)}, bf16[4,512,128]{2,1,0:T(8,128)(2,1)}, ...), condition=%wide.region_5.6_spmd.clone, body=%wide.region_3.0_spmd.clone.sunk | while | flops 2169732608 | bytes 28610700 | solution.py:53
  203.7 9.1 exponential_convert_fusion.2
  212.8 11.9 %convolution_add_fusion.2 = f32[64,8192]{1,0:T(8,128)S(1)} fusion(bf16[512,8192]{1,0:T(8,128)(2,1)} %exponential_convert_fusion.2, f32[64,8192]{1,0:T(8,128)S(1)} %get-tuple-element.123, pred[]{:T(512)S(6)} %compare.3, bf16[64,8192]{1,0:T(8,128)(2,1)S(1)} %copy-done.1), kind=kOutput, calls=%fused_computation.1.clone.1 | convolution fusion | flops 1074823168 | bytes 13631489 | tf_op jit(solution)/shard_map/while/body/eval_jaxpr/dot_general | solution.py:51
  225.7 9.0 exponential_convert_fusion.2
  234.8 11.9 %convolution_add_fusion.2 = f32[64,8192]{1,0:T(8,128)S(1)} fusion(bf16[512,8192]{1,0:T(8,128)(2,1)} %exponential_convert_fusion.2, f32[64,8192]{1,0:T(8,128)S(1)} %get-tuple-element.123, pred[]{:T(512)S(6)} %compare.3, bf16[64,8192]{1,0:T(8,128)(2,1)S(1)} %copy-done.1), kind=kOutput, calls=%fused_computation.1.clone.1 | convolution fusion | flops 1074823168 | bytes 13631489 | tf_op jit(solution)/shard_map/while/body/eval_jaxpr/dot_general | solution.py:51
  247.7 9.0 exponential_convert_fusion.2
  256.8 11.9 %convolution_add_fusion.2 = f32[64,8192]{1,0:T(8,128)S(1)} fusion(bf16[512,8192]{1,0:T(8,128)(2,1)} %exponential_convert_fusion.2, f32[64,8192]{1,0:T(8,128)S(1)} %get-tuple-element.123, pred[]{:T(512)S(6)} %compare.3, bf16[64,8192]{1,0:T(8,128)(2,1)S(1)} %copy-done.1), kind=kOutput, calls=%fused_computation.1.clone.1 | convolution fusion | flops 1074823168 | bytes 13631489 | tf_op jit(solution)/shard_map/while/body/eval_jaxpr/dot_general | solution.py:51
  269.7 9.0 exponential_convert_fusion.2
  278.7 11.9 %convolution_add_fusion.2 = f32[64,8192]{1,0:T(8,128)S(1)} fusion(bf16[512,8192]{1,0:T(8,128)(2,1)} %exponential_convert_fusion.2, f32[64,8192]{1,0:T(8,128)S(1)} %get-tuple-element.123, pred[]{:T(512)S(6)} %compare.3, bf16[64,8192]{1,0:T(8,128)(2,1)S(1)} %copy-done.1), kind=kOutput, calls=%fused_computation.1.clone.1 | convolution fusion | flops 1074823168 | bytes 13631489 | tf_op jit(solution)/shard_map/while/body/eval_jaxpr/dot_general | solution.py:51
  292.0 282.9 %all-reduce.4.cloned.1.call-done = f32[64,8192]{1,0:T(8,128)} async-done(((f32[64,8192]{1,0:T(8,128)}), f32[64,8192]{1,0:T(8,128)}) %all-reduce.4.cloned.1.call-update) | async-done | bytes 2097168 | tf_op jit(solution)/shard_map/psum | solution.py:56
  574.9 105.8 %all-reduce.5 = bf16[64,8192]{1,0:T(8,128)(2,1)S(1)} all-reduce(f32[64,8192]{1,0:T(8,128)} %all-reduce.4.cloned.1.call-done), channel_id=1, replica_groups=mesh['grp'=8,'row'=32] {'grp'}, use_global_device_ids=true, to_apply=%region_7.8 | all-reduce | flops 524288 | bytes 3145728 | tf_op jit(solution)/shard_map/psum | solution.py:56
  680.7 4.4 fusion.3
  685.2 149.8 %reduce-scatter.3.cloned.1.call-done = f32[64,256]{1,0:T(8,128)} async-done(((f32[64,8192]{1,0:T(8,128)}), f32[64,256]{1,0:T(8,128)}) %reduce-scatter.3.cloned.1.call-update) | async-done | bytes 65552 | tf_op jit(solution)/shard_map/reduce_scatter | solution.py:62
  835.0 4.5 fusion.4
  839.6 144.8 %reduce-scatter.5.cloned.1.call-done = f32[64,256]{1,0:T(8,128)} async-done(((f32[64,8192]{1,0:T(8,128)}), f32[64,256]{1,0:T(8,128)}) %reduce-scatter.5.cloned.1.call-update) | async-done | bytes 65552 | tf_op jit(solution)/shard_map/reduce_scatter | solution.py:67
  985.4 72.6 %all-reduce = (f32[64]{0:T(128)S(1)}, f32[64]{0:T(128)S(1)}) all-reduce(f32[64]{0:T(128)S(1)} %multiply_reduce_fusion.4, f32[64]{0:T(128)S(1)} %multiply_reduce_fusion.3), channel_id=1, replica_groups=mesh['grp'=8,'row'=32] {'row'}, use_global_device_ids=true, to_apply=%region_1.2 | all-reduce | flops 128 | bytes 1024 | tf_op jit(solution)/shard_map/psum | solution.py:68
  1059.0 67.8 %psum.39 = f32[64]{0:T(128)S(1)} all-reduce(f32[64]{0:T(128)S(1)} %get-tuple-element.71), channel_id=1, replica_groups=mesh['grp'=8,'row'=32] {'row'}, use_global_device_ids=true, to_apply=%region_13.14 | all-reduce | flops 64 | bytes 512 | tf_op jit(solution)/shard_map/psum | solution.py:72
  (41 shorter events, 8.7 us)
Async XLA Ops:
  7.2 67.6 %all-gather.4.cloned.1.call-start = ((), (), s32[]{:S(2)}) async-start(), calls=%async_computation.2 | async-start | bytes 1081344 | tf_op jit(solution)/shard_map/all_gather | solution.py:26
  8.7 130.0 %all-gather.6.cloned.1.call-start = ((), (), s32[]{:S(2)}) async-start(), calls=%async_computation.3 | async-start | bytes 1081344 | tf_op jit(solution)/shard_map/all_gather | solution.py:34
  79.3 123.4 %all-gather.8.cloned.1.call-start = ((), (), s32[]{:S(2)}) async-start(), calls=%async_computation.4 | async-start | bytes 1081344 | tf_op jit(solution)/shard_map/all_gather | solution.py:39
  143.3 431.6 %all-reduce.4.cloned.1.call-start = ((), (), s32[]{:S(2)}) async-start(), calls=%async_computation.5 | async-start | bytes 4194304 | tf_op jit(solution)/shard_map/psum | solution.py:56
  203.7 9.1 copy-start.1
  225.7 9.1 copy-start.1
  247.7 9.1 copy-start.1
  269.7 9.1 copy-start.1
  290.6 1.3 copy-start
  291.9 543.1 %reduce-scatter.3.cloned.1.call-start = ((), (), s32[]{:S(2)}) async-start(), calls=%async_computation.6 | async-start | bytes 2162688 | tf_op jit(solution)/shard_map/reduce_scatter | solution.py:62
  685.1 299.3 %reduce-scatter.5.cloned.1.call-start = ((), (), s32[]{:S(2)}) async-start(), calls=%async_computation.7 | async-start | bytes 2162688 | tf_op jit(solution)/shard_map/reduce_scatter | solution.py:67
  835.0 4.5 copy-start.4
  835.0 149.4 %copy-start.2 = (f32[64,256]{1,0:T(8,128)S(1)}, f32[64,256]{1,0:T(8,128)}, u32[]{:S(2)}) copy-start(f32[64,256]{1,0:T(8,128)} %param.15) | copy-start | bytes 196612
  835.0 291.9 %copy-start.5 = (f32[64,256]{1,0:T(8,128)S(1)}, f32[64,256]{1,0:T(8,128)}, u32[]{:S(2)}) copy-start(f32[64,256]{1,0:T(8,128)} %param.13) | copy-start | bytes 196612
  1059.0 68.6 %copy-start.3 = (f32[64,256]{1,0:T(8,128)}, f32[64,256]{1,0:T(8,128)S(1)}, u32[]{:S(2)}) copy-start(f32[64,256]{1,0:T(8,128)S(1)} %get-tuple-element.72) | copy-start | bytes 196612
Sparse Core Ops, SparseCore 0:
  10.3 64.4 all-gather.3
  79.4 59.2 all-gather.5
  143.4 59.2 all-gather.7
  292.1 282.7 all-reduce.3
  685.3 149.6 reduce-scatter.2
  839.6 144.7 reduce-scatter.4
